TPU v7x, 32 devices: a whole 2x2x4 slice. The times are simulated.
32 devices in a mesh: section: 2 (over y), tensor: 4 (over z), fsdp: 4 (over x, core).
Axes of the slice: x: 2, y: 2, z: 4, core: 2. Of those that a mesh axis runs over, the one named last changes fastest.
Arguments:
- images: bfloat16 [2, 4, 729, 1152], P(None, 'fsdp'), may hold values from -6 to 6
- cotangent: bfloat16 [2, 4, 729, 1152], P(None, 'fsdp'), may hold values from -6 to 6
- qkv_weight: bfloat16 [2, 3, 1152, 1152], P('section', None, 'fsdp', 'tensor'), may hold values from -1 to 1
- qv_bias: bfloat16 [2, 2, 1152], P('section', None, 'tensor'), may hold values from -3 to 3
- out_weight: bfloat16 [2, 1152, 1152], P('section', 'tensor', 'fsdp'), may hold values from -0.75 to 0.75
- up_weight: bfloat16 [2, 1152, 4304], P('section', 'fsdp', 'tensor'), may hold values from -0.1875 to 0.1875
- up_bias: bfloat16 [2, 4304], P('section', 'tensor'), may hold values from -3 to 3
- down_weight: bfloat16 [2, 4304, 1152], P('section', 'tensor', 'fsdp'), may hold values from -0.09375 to 0.09375
- gains: bfloat16 [2, 2, 1152], P('section', None, 'fsdp'), may hold values from 0.099609375 to 1.8984375
- shifts: bfloat16 [2, 4, 1152], P('section', None, 'fsdp'), may hold values from -3 to 3
Outputs:
- section_outputs: bfloat16 [2, 2, 4, 729, 1152], P('section', None, 'fsdp')
- input_grads: bfloat16 [2, 2, 4, 729, 1152], P('section', None, 'fsdp')
- grad_qkv: float32 [2, 3, 1152, 1152], P('section', None, 'fsdp', 'tensor')
- grad_qv_bias: float32 [2, 2, 1152], P('section', None, 'tensor')
- grad_out: float32 [2, 1152, 1152], P('section', 'tensor', 'fsdp')
- grad_up: float32 [2, 1152, 4304], P('section', 'fsdp', 'tensor')
- grad_up_bias: float32 [2, 4304], P('section', 'tensor')
- grad_down: float32 [2, 4304, 1152], P('section', 'tensor', 'fsdp')
- grad_gains: float32 [2, 2, 1152], P('section', None, 'fsdp')
- grad_shifts: float32 [2, 4, 1152], P('section', None, 'fsdp')
All inputs are finite; a program needn't handle non-finite values.
Results may differ from a plain program's by a relative error of at most 0.013.
Values may be sent and summed in bfloat16 or wider, within the bound.
A program may use at most 256 MiB of HBM per device.

v0:
```python
import jax
import jax.numpy as jnp
from jax import lax
from jax.sharding import PartitionSpec as P

HD = 72
NORM_EPS = 1e-06
GELU_ROOT = 0.7978845608028654
GELU_CUBIC = 0.044715


def from_behind(value, axis, steps):
    count = lax.axis_size(axis)
    leading, last = (max(0, -steps), min(count, count - steps))
    return lax.ppermute(value, axis, [(source, source + steps) for source in range(leading, last)])


def gelu_value(value):
    return 0.5 * value * (1.0 + jnp.tanh(GELU_ROOT * (value + GELU_CUBIC * value * value * value)))


def gelu_slope(value):
    inner = jnp.tanh(GELU_ROOT * (value + GELU_CUBIC * value * value * value))
    return 0.5 * (1.0 + inner) + 0.5 * value * (1.0 - inner * inner) * GELU_ROOT * (
        1.0 + 3.0 * GELU_CUBIC * value * value
    )


def norm_forward(token_rows, gain, shift):
    mean_row = jnp.mean(token_rows, axis=-1, keepdims=True)
    centred = token_rows - mean_row
    inverse = lax.rsqrt(jnp.mean(centred * centred, axis=-1, keepdims=True) + NORM_EPS)
    normed = centred * inverse
    return (normed * gain + shift, normed, inverse)


def norm_backward(grad_normed, normed, inverse, gain):
    scaled = grad_normed * gain
    inner = (
        scaled
        - jnp.mean(scaled, axis=-1, keepdims=True)
        - normed * jnp.mean(scaled * normed, axis=-1, keepdims=True)
    )
    return (inverse * inner, jnp.sum(grad_normed * normed, axis=0), jnp.sum(grad_normed, axis=0))


def layer_forward(layer_input, weights, qv_bias, up_bias):
    qkv_weight, out_weight, up_weight, down_weight, gains, shifts = weights
    image_count, seq_len, model_width = layer_input.shape
    local_heads = qkv_weight.shape[2] // HD
    score_scale = HD ** (-0.5)
    gain_rows = gains.astype(jnp.float32)
    shift_rows = shifts.astype(jnp.float32)
    token_rows = layer_input.astype(jnp.float32).reshape(-1, model_width)
    normed_one = norm_forward(token_rows, gain_rows[0], shift_rows[0])[0].astype(jnp.bfloat16)
    projected = jnp.einsum(
        "td,cde->cte", normed_one, qkv_weight, preferred_element_type=jnp.float32
    )
    bias_rows = qv_bias.astype(jnp.float32)
    queries = (projected[0] + bias_rows[0]).astype(jnp.bfloat16)
    key_rows = projected[1].astype(jnp.bfloat16)
    values = (projected[2] + bias_rows[1]).astype(jnp.bfloat16)
    head_shape = (image_count, seq_len, local_heads, HD)
    scores = (
        jnp.einsum(
            "bqhd,bkhd->bhqk",
            queries.reshape(head_shape),
            key_rows.reshape(head_shape),
            preferred_element_type=jnp.float32,
        )
        * score_scale
    )
    row_max = jnp.max(scores, axis=-1, keepdims=True)
    exp_scores = jnp.exp(scores - row_max)
    row_total = jnp.sum(exp_scores, axis=-1, keepdims=True)
    attn_probs = (exp_scores / row_total).astype(jnp.bfloat16)
    log_total = row_max + jnp.log(row_total)
    context = jnp.einsum(
        "bhqk,bkhd->bqhd",
        attn_probs,
        values.reshape(head_shape),
        preferred_element_type=jnp.float32,
    )
    context = context.astype(jnp.bfloat16).reshape(-1, local_heads * HD)
    attn_term = jnp.dot(context, out_weight, preferred_element_type=jnp.float32)
    hidden = token_rows + lax.psum(attn_term, "tensor") + shift_rows[1]
    normed_two = norm_forward(hidden, gain_rows[1], shift_rows[2])[0].astype(jnp.bfloat16)
    pre_act = jnp.dot(normed_two, up_weight, preferred_element_type=jnp.float32) + up_bias.astype(
        jnp.float32
    )
    active = gelu_value(pre_act).astype(jnp.bfloat16)
    mlp_term = jnp.dot(active, down_weight, preferred_element_type=jnp.float32)
    output_low = (hidden + lax.psum(mlp_term, "tensor") + shift_rows[3]).astype(jnp.bfloat16)
    stored = (
        layer_input,
        normed_one,
        queries,
        key_rows,
        values,
        log_total,
        context,
        hidden,
        normed_two,
        pre_act,
        active,
    )
    return (output_low, stored)


def layer_backward(grad_output, stored, weights):
    qkv_weight, out_weight, up_weight, down_weight, gains, shifts = weights
    (
        layer_input,
        normed_one,
        queries,
        key_rows,
        values,
        log_total,
        context,
        hidden,
        normed_two,
        pre_act,
        active,
    ) = stored
    image_count, seq_len, model_width = layer_input.shape
    local_heads = qkv_weight.shape[2] // HD
    score_scale = HD ** (-0.5)
    gain_rows = gains.astype(jnp.float32)
    shift_rows = shifts.astype(jnp.float32)
    grad_mix = grad_output.astype(jnp.bfloat16)
    grad_down = jnp.einsum("tf,td->fd", active, grad_mix, preferred_element_type=jnp.float32)
    grad_active = jnp.einsum("td,fd->tf", grad_mix, down_weight, preferred_element_type=jnp.float32)
    grad_pre = (grad_active * gelu_slope(pre_act)).astype(jnp.bfloat16)
    grad_up = jnp.einsum("td,tf->df", normed_two, grad_pre, preferred_element_type=jnp.float32)
    up_bias_grad = jnp.sum(grad_pre.astype(jnp.float32), axis=0)
    two_term = jnp.einsum("tf,df->td", grad_pre, up_weight, preferred_element_type=jnp.float32)
    centred_two, inverse_two = norm_forward(hidden, gain_rows[1], shift_rows[2])[1:]
    grad_normed_two = lax.psum(two_term, "tensor")
    from_two, gain_two_grad, shift_two_grad = norm_backward(
        grad_normed_two, centred_two, inverse_two, gain_rows[1]
    )
    grad_hidden = grad_output + from_two
    grad_attn = grad_hidden.astype(jnp.bfloat16)
    attn_shift_grad = jnp.sum(grad_attn.astype(jnp.float32), axis=0)
    mix_shift_grad = jnp.sum(grad_mix.astype(jnp.float32), axis=0)
    grad_out = jnp.einsum("te,td->ed", context, grad_attn, preferred_element_type=jnp.float32)
    grad_context = jnp.einsum(
        "td,ed->te", grad_attn, out_weight, preferred_element_type=jnp.float32
    ).astype(jnp.bfloat16)
    head_shape = (image_count, seq_len, local_heads, HD)
    query_heads = queries.reshape(head_shape)
    key_heads = key_rows.reshape(head_shape)
    value_heads = values.reshape(head_shape)
    context_grads = grad_context.reshape(head_shape)
    scores = (
        jnp.einsum("bqhd,bkhd->bhqk", query_heads, key_heads, preferred_element_type=jnp.float32)
        * score_scale
    )
    probs_full = jnp.exp(scores - log_total)
    mixed = jnp.einsum(
        "bqhd,bkhd->bhqk", context_grads, value_heads, preferred_element_type=jnp.float32
    )
    row_delta = jnp.sum(mixed * probs_full, axis=-1, keepdims=True)
    grad_scores = (probs_full * (mixed - row_delta)).astype(jnp.bfloat16)
    grad_values = jnp.einsum(
        "bhqk,bqhd->bkhd",
        probs_full.astype(jnp.bfloat16),
        context_grads,
        preferred_element_type=jnp.float32,
    ).astype(jnp.bfloat16)
    grad_queries = (
        jnp.einsum("bhqk,bkhd->bqhd", grad_scores, key_heads, preferred_element_type=jnp.float32)
        * score_scale
    ).astype(jnp.bfloat16)
    grad_keys = (
        jnp.einsum("bhqk,bqhd->bkhd", grad_scores, query_heads, preferred_element_type=jnp.float32)
        * score_scale
    ).astype(jnp.bfloat16)
    flat_shape = (-1, local_heads * HD)
    grad_proj = jnp.stack(
        [
            grad_queries.reshape(flat_shape),
            grad_keys.reshape(flat_shape),
            grad_values.reshape(flat_shape),
        ]
    )
    grad_qkv = jnp.einsum("td,cte->cde", normed_one, grad_proj, preferred_element_type=jnp.float32)
    qv_bias_grad = jnp.stack(
        [
            jnp.sum(grad_proj[0].astype(jnp.float32), axis=0),
            jnp.sum(grad_proj[2].astype(jnp.float32), axis=0),
        ]
    )
    one_term = jnp.einsum("cte,cde->td", grad_proj, qkv_weight, preferred_element_type=jnp.float32)
    token_rows = layer_input.astype(jnp.float32).reshape(-1, model_width)
    grad_normed_one = lax.psum(one_term, "tensor")
    centred_one, inverse_one = norm_forward(token_rows, gain_rows[0], shift_rows[0])[1:]
    from_one, gain_one_grad, shift_one_grad = norm_backward(
        grad_normed_one, centred_one, inverse_one, gain_rows[0]
    )
    grad_low = (grad_hidden + from_one).astype(jnp.bfloat16)
    grad_gains = jnp.stack([gain_one_grad, gain_two_grad])
    grad_shifts = jnp.stack([shift_one_grad, attn_shift_grad, shift_two_grad, mix_shift_grad])
    return (
        grad_low,
        (grad_qkv, grad_out, grad_up, grad_down, grad_gains, grad_shifts),
        (qv_bias_grad, up_bias_grad),
    )


def per_device(
    images,
    cotangent,
    qkv_weight,
    qv_bias,
    out_weight,
    up_weight,
    up_bias,
    down_weight,
    gains,
    shifts,
):
    micro_count, image_count, seq_len, model_width = images.shape
    section_index = lax.axis_index("section")
    local_qv = qv_bias[0]
    local_up = up_bias[0]
    weights = (
        lax.all_gather(qkv_weight[0], "fsdp", axis=1, tiled=True),
        lax.all_gather(out_weight[0], "fsdp", axis=1, tiled=True),
        lax.all_gather(up_weight[0], "fsdp", axis=0, tiled=True),
        lax.all_gather(down_weight[0], "fsdp", axis=1, tiled=True),
        lax.all_gather(gains[0], "fsdp", axis=1, tiled=True),
        lax.all_gather(shifts[0], "fsdp", axis=1, tiled=True),
    )

    def forward_tick(carried, tick_index):
        own_input = lax.dynamic_index_in_dim(
            images, jnp.minimum(tick_index, micro_count - 1), 0, keepdims=False
        )
        layer_input = jnp.where(section_index == 0, own_input, carried)
        output_low, stored = layer_forward(layer_input, weights, local_qv, local_up)
        output_low = output_low.reshape(image_count, seq_len, model_width)
        passed = from_behind(output_low, "section", 1)
        return (passed, (output_low, stored))

    ticks = jnp.arange(micro_count + 1, dtype=jnp.int32)
    output_all, stored_all = lax.scan(forward_tick, jnp.zeros_like(images[0]), ticks)[1]
    section_outputs = lax.dynamic_slice_in_dim(output_all, section_index, micro_count, 0)
    start_sums = tuple((jnp.zeros(item.shape, jnp.float32) for item in weights))
    start_biases = (jnp.zeros(local_qv.shape, jnp.float32), jnp.zeros(local_up.shape, jnp.float32))

    def backward_tick(carry, tick_index):
        received, grad_sums, bias_totals = carry
        micro_index = micro_count - tick_index - section_index
        is_valid = (micro_index >= 0) & (micro_index < micro_count)
        safe_index = jnp.clip(micro_index, 0, micro_count - 1)
        own_grad = (
            lax.dynamic_index_in_dim(cotangent, safe_index, 0, keepdims=False)
            .astype(jnp.float32)
            .reshape(-1, model_width)
        )
        grad_output = jnp.where(section_index == 1, own_grad, received)
        stored = tuple(
            (
                lax.dynamic_index_in_dim(item, safe_index + section_index, 0, keepdims=False)
                for item in stored_all
            )
        )
        grad_low, grads, biases = layer_backward(grad_output, stored, weights)
        grads = tuple((jnp.where(is_valid, item, 0.0) for item in grads))
        biases = tuple((jnp.where(is_valid, item, 0.0) for item in biases))
        grad_low = grad_low.reshape(image_count, seq_len, model_width)
        passed = from_behind(grad_low, "section", -1).astype(jnp.float32).reshape(-1, model_width)
        grad_sums = tuple((first + second for first, second in zip(grad_sums, grads)))
        bias_totals = tuple((first + second for first, second in zip(bias_totals, biases)))
        return ((passed, grad_sums, bias_totals), grad_low)

    start_grad = jnp.zeros((image_count * seq_len, model_width), jnp.float32)
    finished, grad_all = lax.scan(backward_tick, (start_grad, start_sums, start_biases), ticks)
    grad_sums, bias_totals = (finished[1], finished[2])
    final_grads = (
        lax.psum_scatter(
            grad_sums[0].astype(jnp.bfloat16), "fsdp", scatter_dimension=1, tiled=True
        ).astype(jnp.float32),
        lax.psum_scatter(
            grad_sums[1].astype(jnp.bfloat16), "fsdp", scatter_dimension=1, tiled=True
        ).astype(jnp.float32),
        lax.psum_scatter(
            grad_sums[2].astype(jnp.bfloat16), "fsdp", scatter_dimension=0, tiled=True
        ).astype(jnp.float32),
        lax.psum_scatter(
            grad_sums[3].astype(jnp.bfloat16), "fsdp", scatter_dimension=1, tiled=True
        ).astype(jnp.float32),
        lax.psum_scatter(
            grad_sums[4].astype(jnp.bfloat16), "fsdp", scatter_dimension=1, tiled=True
        ).astype(jnp.float32),
        lax.psum_scatter(
            grad_sums[5].astype(jnp.bfloat16), "fsdp", scatter_dimension=1, tiled=True
        ).astype(jnp.float32),
    )
    final_biases = lax.psum((bias_totals[0], bias_totals[1]), "fsdp")
    gain_grads, shift_grads = (final_grads[4], final_grads[5])
    input_grads = jnp.flip(lax.dynamic_slice_in_dim(grad_all, 1 - section_index, micro_count, 0), 0)
    return (
        section_outputs[None],
        input_grads[None],
        final_grads[0][None],
        final_biases[0][None],
        final_grads[1][None],
        final_grads[2][None],
        final_biases[1][None],
        final_grads[3][None],
        gain_grads[None],
        shift_grads[None],
    )


def solution(mesh):
    return jax.shard_map(
        per_device,
        mesh=mesh,
        in_specs=(
            P(None, "fsdp", None, None),
            P(None, "fsdp", None, None),
            P("section", None, "fsdp", "tensor"),
            P("section", None, "tensor"),
            P("section", "tensor", "fsdp"),
            P("section", "fsdp", "tensor"),
            P("section", "tensor"),
            P("section", "tensor", "fsdp"),
            P("section", None, "fsdp"),
            P("section", None, "fsdp"),
        ),
        out_specs=(
            P("section", None, "fsdp", None, None),
            P("section", None, "fsdp", None, None),
            P("section", None, "fsdp", "tensor"),
            P("section", None, "tensor"),
            P("section", "tensor", "fsdp"),
            P("section", "fsdp", "tensor"),
            P("section", "tensor"),
            P("section", "tensor", "fsdp"),
            P("section", None, "fsdp"),
            P("section", None, "fsdp"),
        ),
        check_vma=False,
    )
```

profile of v0, /device:TPU:0, one launch (start us, length us, event | category | flops | bytes accessed | tf_op | source)
XLA Modules:
  0.0 2444.3 jit_solution(16826438468239682339)
XLA Ops:
  83.8 22.2 all-gather.12.cloned.1.call-done
  112.5 1034.5 %while.66 = (s32[]{:T(128)}, bf16[1,729,1152]{2,1,0:T(8,128)(2,1)}, bf16[3,1,729,1152]{3,2,1,0:T(8,128)(2,1)}, bf16[3,1,729,1152]{3,2,1,0:T(8,128)(2,1)}, bf16[3...) while((s32[]{:T(128)}, bf16[1,729,1152]{2,1,0:T(8,128)(2,1)}, ...), condition=%wide.region_9.10_spmd, body=%wide.region_0.9_spmd.sunk | while | flops 6232035840 | bytes 263704656 | solution.py:247
  145.6 130.7 %all-reduce.6.cloned.1.call-done = f32[729,1152]{1,0:T(8,128)} async-done(((f32[729,1152]{1,0:T(8,128)}), f32[729,1152]{1,0:T(8,128)}) %all-reduce.6.cloned.1.call-update) | async-done | bytes 3359248 | tf_op jit(solution)/shard_map/while/body/eval_jaxpr/psum | solution.py:86
  297.6 124.3 %all-reduce.8.cloned.1.call-done = f32[729,1152]{1,0:T(8,128)} async-done(((f32[729,1152]{1,0:T(8,128)}), f32[729,1152]{1,0:T(8,128)}) %all-reduce.8.cloned.1.call-update) | async-done | bytes 3359248 | tf_op jit(solution)/shard_map/while/body/eval_jaxpr/psum | solution.py:93
  436.2 29.8 %collective-permute-done = bf16[1,729,1152]{2,1,0:T(8,128)(2,1)} collective-permute-done((bf16[1,729,1152]{2,1,0:T(8,128)(2,1)}, bf16[1,729,1152]{2,1,0:T(8,128)(2,1)}, u32[]{:S(2)}, u32[]{:S(2)}) %collective-permute-start) | collective-permute-done | bytes 1679648 | tf_op jit(solution)/shard_map/while/body/eval_jaxpr/ppermute | solution.py:15
  486.1 130.8 %all-reduce.6.cloned.1.call-done = f32[729,1152]{1,0:T(8,128)} async-done(((f32[729,1152]{1,0:T(8,128)}), f32[729,1152]{1,0:T(8,128)}) %all-reduce.6.cloned.1.call-update) | async-done | bytes 3359248 | tf_op jit(solution)/shard_map/while/body/eval_jaxpr/psum | solution.py:86
  638.1 124.4 %all-reduce.8.cloned.1.call-done = f32[729,1152]{1,0:T(8,128)} async-done(((f32[729,1152]{1,0:T(8,128)}), f32[729,1152]{1,0:T(8,128)}) %all-reduce.8.cloned.1.call-update) | async-done | bytes 3359248 | tf_op jit(solution)/shard_map/while/body/eval_jaxpr/psum | solution.py:93
  776.8 29.7 %collective-permute-done = bf16[1,729,1152]{2,1,0:T(8,128)(2,1)} collective-permute-done((bf16[1,729,1152]{2,1,0:T(8,128)(2,1)}, bf16[1,729,1152]{2,1,0:T(8,128)(2,1)}, u32[]{:S(2)}, u32[]{:S(2)}) %collective-permute-start) | collective-permute-done | bytes 1679648 | tf_op jit(solution)/shard_map/while/body/eval_jaxpr/ppermute | solution.py:15
  826.6 130.8 %all-reduce.6.cloned.1.call-done = f32[729,1152]{1,0:T(8,128)} async-done(((f32[729,1152]{1,0:T(8,128)}), f32[729,1152]{1,0:T(8,128)}) %all-reduce.6.cloned.1.call-update) | async-done | bytes 3359248 | tf_op jit(solution)/shard_map/while/body/eval_jaxpr/psum | solution.py:86
  978.7 124.3 %all-reduce.8.cloned.1.call-done = f32[729,1152]{1,0:T(8,128)} async-done(((f32[729,1152]{1,0:T(8,128)}), f32[729,1152]{1,0:T(8,128)}) %all-reduce.8.cloned.1.call-update) | async-done | bytes 3359248 | tf_op jit(solution)/shard_map/while/body/eval_jaxpr/psum | solution.py:93
  1117.1 29.7 %collective-permute-done = bf16[1,729,1152]{2,1,0:T(8,128)(2,1)} collective-permute-done((bf16[1,729,1152]{2,1,0:T(8,128)(2,1)}, bf16[1,729,1152]{2,1,0:T(8,128)(2,1)}, u32[]{:S(2)}, u32[]{:S(2)}) %collective-permute-start) | collective-permute-done | bytes 1679648 | tf_op jit(solution)/shard_map/while/body/eval_jaxpr/ppermute | solution.py:15
  1149.9 1104.1 %while.67 = (s32[]{:T(128)}, f32[729,1152]{1,0:T(8,128)S(1)}, f32[3,1152,288]{1,2,0:T(8,128)}, f32[288,1152]{1,0:T(8,128)}, f32[1152,1076]{0,1:T(8,128)}, /*inde...) while((s32[]{:T(128)}, f32[729,1152]{1,0:T(8,128)S(1)}, ...), condition=%wide.region_31.32_spmd.clone, body=%wide.region_10.31_spmd.clone.sunk | while | flops 12738733056 | bytes 490833920 | solution.py:279
  1200.5 115.7 %all-reduce.10.cloned.1.call-done = f32[729,1152]{1,0:T(8,128)} async-done(((f32[729,1152]{1,0:T(8,128)}), f32[729,1152]{1,0:T(8,128)}) %all-reduce.10.cloned.1.call-update) | async-done | bytes 3359248 | tf_op jit(solution)/shard_map/while/body/eval_jaxpr/psum | solution.py:138
  1378.7 106.2 %all-reduce.12.cloned.1.call-done = f32[729,1152]{1,0:T(8,128)} async-done(((f32[729,1152]{1,0:T(8,128)}), f32[729,1152]{1,0:T(8,128)}) %all-reduce.12.cloned.1.call-update) | async-done | bytes 3359248 | tf_op jit(solution)/shard_map/while/body/eval_jaxpr/psum | solution.py:196
  1498.5 34.7 %collective-permute-done.1 = bf16[1,729,1152]{2,1,0:T(8,128)(2,1)S(1)} collective-permute-done((bf16[1,729,1152]{2,1,0:T(8,128)(2,1)S(1)}, bf16[1,729,1152]{2,1,0:T(8,128)(2,1)S(1)}, u32[]{:S(2)}, u32[]{:S(2)}) %collective-permute-start.1) | collective-permute-done | bytes 1679648 | tf_op jit(solution)/shard_map/while/body/eval_jaxpr/ppermute | solution.py:15
  1562.8 113.6 %all-reduce.10.cloned.1.call-done = f32[729,1152]{1,0:T(8,128)} async-done(((f32[729,1152]{1,0:T(8,128)}), f32[729,1152]{1,0:T(8,128)}) %all-reduce.10.cloned.1.call-update) | async-done | bytes 3359248 | tf_op jit(solution)/shard_map/while/body/eval_jaxpr/psum | solution.py:138
  1740.9 104.2 %all-reduce.12.cloned.1.call-done = f32[729,1152]{1,0:T(8,128)} async-done(((f32[729,1152]{1,0:T(8,128)}), f32[729,1152]{1,0:T(8,128)}) %all-reduce.12.cloned.1.call-update) | async-done | bytes 3359248 | tf_op jit(solution)/shard_map/while/body/eval_jaxpr/psum | solution.py:196
  1858.7 34.7 %collective-permute-done.1 = bf16[1,729,1152]{2,1,0:T(8,128)(2,1)S(1)} collective-permute-done((bf16[1,729,1152]{2,1,0:T(8,128)(2,1)S(1)}, bf16[1,729,1152]{2,1,0:T(8,128)(2,1)S(1)}, u32[]{:S(2)}, u32[]{:S(2)}) %collective-permute-start.1) | collective-permute-done | bytes 1679648 | tf_op jit(solution)/shard_map/while/body/eval_jaxpr/ppermute | solution.py:15
  1922.9 113.6 %all-reduce.10.cloned.1.call-done = f32[729,1152]{1,0:T(8,128)} async-done(((f32[729,1152]{1,0:T(8,128)}), f32[729,1152]{1,0:T(8,128)}) %all-reduce.10.cloned.1.call-update) | async-done | bytes 3359248 | tf_op jit(solution)/shard_map/while/body/eval_jaxpr/psum | solution.py:138
  2100.9 104.2 %all-reduce.12.cloned.1.call-done = f32[729,1152]{1,0:T(8,128)} async-done(((f32[729,1152]{1,0:T(8,128)}), f32[729,1152]{1,0:T(8,128)}) %all-reduce.12.cloned.1.call-update) | async-done | bytes 3359248 | tf_op jit(solution)/shard_map/while/body/eval_jaxpr/psum | solution.py:196
  2218.7 34.7 %collective-permute-done.1 = bf16[1,729,1152]{2,1,0:T(8,128)(2,1)S(1)} collective-permute-done((bf16[1,729,1152]{2,1,0:T(8,128)(2,1)S(1)}, bf16[1,729,1152]{2,1,0:T(8,128)(2,1)S(1)}, u32[]{:S(2)}, u32[]{:S(2)}) %collective-permute-start.1) | collective-permute-done | bytes 1679648 | tf_op jit(solution)/shard_map/while/body/eval_jaxpr/ppermute | solution.py:15
  2296.5 31.6 %rev.4 = bf16[2,1,729,1152]{3,0,2,1:T(2,128)(2,1)} reverse(bf16[2,1,729,1152]{3,0,2,1:T(2,128)(2,1)} %constant_dynamic-slice_fusion.3), dimensions={0} | reverse | bytes 6718464 | tf_op jit(solution)/shard_map/jit(_flip)/rev | solution.py:303
  2364.7 32.0 %reduce-scatter.23.cloned.1.call-done = bf16[288,1076]{1,0:T(8,128)(2,1)} async-done(((bf16[1152,1076]{1,0:T(8,128)(2,1)}), bf16[288,1076]{1,0:T(8,128)(2,1)}) %reduce-scatter.23.cloned.1.call-update) | async-done | bytes 619792
  2399.9 34.1 %reduce-scatter.25.cloned.1.call-done = bf16[288,1076]{1,0:T(8,128)(2,1)} async-done(((bf16[1152,1076]{1,0:T(8,128)(2,1)}), bf16[288,1076]{1,0:T(8,128)(2,1)}) %reduce-scatter.25.cloned.1.call-update) | async-done | bytes 619792
  (798 shorter events, 651.7 us)
Async XLA Ops:
  7.2 58.4 %all-gather.10.cloned.1.call-start = ((), (), s32[]{:S(2)}) async-start(), calls=%async_computation.6 | async-start | bytes 4423680 | tf_op jit(solution)/shard_map/all_gather | solution.py:228
  9.8 68.9 %all-gather.14.cloned.1.call-start = ((), (), s32[]{:S(2)}) async-start(), calls=%async_computation.8 | async-start | bytes 3317760 | tf_op jit(solution)/shard_map/all_gather | solution.py:231
  10.5 95.4 %all-gather.12.cloned.1.call-start = ((), (), s32[]{:S(2)}) async-start(), calls=%async_computation.7 | async-start | bytes 3317760 | tf_op jit(solution)/shard_map/all_gather | solution.py:230
  125.5 150.8 %all-reduce.6.cloned.1.call-start = ((), (), s32[]{:S(2)}) async-start(), calls=%async_computation.15 | async-start | bytes 6782976 | tf_op jit(solution)/shard_map/while/body/eval_jaxpr/psum | solution.py:86
  145.5 276.4 %all-reduce.8.cloned.1.call-start = ((), (), s32[]{:S(2)}) async-start(), calls=%async_computation.16 | async-start | bytes 6782976 | tf_op jit(solution)/shard_map/while/body/eval_jaxpr/psum | solution.py:93
  466.0 150.8 %all-reduce.6.cloned.1.call-start = ((), (), s32[]{:S(2)}) async-start(), calls=%async_computation.15 | async-start | bytes 6782976 | tf_op jit(solution)/shard_map/while/body/eval_jaxpr/psum | solution.py:86
  486.0 276.4 %all-reduce.8.cloned.1.call-start = ((), (), s32[]{:S(2)}) async-start(), calls=%async_computation.16 | async-start | bytes 6782976 | tf_op jit(solution)/shard_map/while/body/eval_jaxpr/psum | solution.py:93
  806.5 150.8 %all-reduce.6.cloned.1.call-start = ((), (), s32[]{:S(2)}) async-start(), calls=%async_computation.15 | async-start | bytes 6782976 | tf_op jit(solution)/shard_map/while/body/eval_jaxpr/psum | solution.py:86
  826.5 276.4 %all-reduce.8.cloned.1.call-start = ((), (), s32[]{:S(2)}) async-start(), calls=%async_computation.16 | async-start | bytes 6782976 | tf_op jit(solution)/shard_map/while/body/eval_jaxpr/psum | solution.py:93
  1171.3 144.9 %all-reduce.10.cloned.1.call-start = ((), (), s32[]{:S(2)}) async-start(), calls=%async_computation.17 | async-start | bytes 6782976 | tf_op jit(solution)/shard_map/while/body/eval_jaxpr/psum | solution.py:138
  1186.8 298.1 %all-reduce.12.cloned.1.call-start = ((), (), s32[]{:S(2)}) async-start(), calls=%async_computation.18 | async-start | bytes 6782976 | tf_op jit(solution)/shard_map/while/body/eval_jaxpr/psum | solution.py:196
  1492.7 40.5 %collective-permute-start.1 = (bf16[1,729,1152]{2,1,0:T(8,128)(2,1)S(1)}, bf16[1,729,1152]{2,1,0:T(8,128)(2,1)S(1)}, u32[]{:S(2)}, u32[]{:S(2)}) collective-permute-start(bf16[1,729,1152]{2,1,0:T(8,128)(2,1)S(1)} %bitcast.382), channel_id=1, source_target_pairs={{16,0},{17,1},{18,2},{19,3},{20,4},{21,5},{22,6},{23,7},{24,8},{25... | collective-permute-start | bytes 5038856 | tf_op jit(solution)/shard_map/while/body/eval_jaxpr/ppermute | solution.py:15
  1533.4 143.0 %all-reduce.10.cloned.1.call-start = ((), (), s32[]{:S(2)}) async-start(), calls=%async_computation.17 | async-start | bytes 6782976 | tf_op jit(solution)/shard_map/while/body/eval_jaxpr/psum | solution.py:138
  1548.9 296.2 %all-reduce.12.cloned.1.call-start = ((), (), s32[]{:S(2)}) async-start(), calls=%async_computation.18 | async-start | bytes 6782976 | tf_op jit(solution)/shard_map/while/body/eval_jaxpr/psum | solution.py:196
  1852.9 40.5 %collective-permute-start.1 = (bf16[1,729,1152]{2,1,0:T(8,128)(2,1)S(1)}, bf16[1,729,1152]{2,1,0:T(8,128)(2,1)S(1)}, u32[]{:S(2)}, u32[]{:S(2)}) collective-permute-start(bf16[1,729,1152]{2,1,0:T(8,128)(2,1)S(1)} %bitcast.382), channel_id=1, source_target_pairs={{16,0},{17,1},{18,2},{19,3},{20,4},{21,5},{22,6},{23,7},{24,8},{25... | collective-permute-start | bytes 5038856 | tf_op jit(solution)/shard_map/while/body/eval_jaxpr/ppermute | solution.py:15
  1893.6 143.0 %all-reduce.10.cloned.1.call-start = ((), (), s32[]{:S(2)}) async-start(), calls=%async_computation.17 | async-start | bytes 6782976 | tf_op jit(solution)/shard_map/while/body/eval_jaxpr/psum | solution.py:138
  1909.1 296.0 %all-reduce.12.cloned.1.call-start = ((), (), s32[]{:S(2)}) async-start(), calls=%async_computation.18 | async-start | bytes 6782976 | tf_op jit(solution)/shard_map/while/body/eval_jaxpr/psum | solution.py:196
  2212.9 40.5 %collective-permute-start.1 = (bf16[1,729,1152]{2,1,0:T(8,128)(2,1)S(1)}, bf16[1,729,1152]{2,1,0:T(8,128)(2,1)S(1)}, u32[]{:S(2)}, u32[]{:S(2)}) collective-permute-start(bf16[1,729,1152]{2,1,0:T(8,128)(2,1)S(1)} %bitcast.382), channel_id=1, source_target_pairs={{16,0},{17,1},{18,2},{19,3},{20,4},{21,5},{22,6},{23,7},{24,8},{25... | collective-permute-start | bytes 5038856 | tf_op jit(solution)/shard_map/while/body/eval_jaxpr/ppermute | solution.py:15
  2254.0 87.3 %reduce-scatter.27.cloned.1.call-start = ((), (), s32[]{:S(2)}) async-start(), calls=%async_computation.13 | async-start | bytes 368640
  2255.0 87.9 %reduce-scatter.29.cloned.1.call-start = ((), (), s32[]{:S(2)}) async-start(), calls=%async_computation.14 | async-start | bytes 368640
  2256.0 88.4 %reduce-scatter.21.cloned.1.call-start = ((), (), s32[]{:S(2)}) async-start(), calls=%async_computation.10 | async-start | bytes 1105920
  2258.7 100.9 %reduce-scatter.19.cloned.1.call-start = ((), (), s32[]{:S(2)}) async-start(), calls=%async_computation.9 | async-start | bytes 2580480
  2272.6 124.2 %reduce-scatter.23.cloned.1.call-start = ((), (), s32[]{:S(2)}) async-start(), calls=%async_computation.11 | async-start | bytes 3317760
  2278.6 155.4 %reduce-scatter.25.cloned.1.call-start = ((), (), s32[]{:S(2)}) async-start(), calls=%async_computation.12 | async-start | bytes 3317760
  (210 other events, 2190.6 us)
Sparse Core Ops, SparseCore 0:
  10.1 40.3 all-gather.9
  52.1 26.5 all-gather.13
  80.2 25.7 all-gather.11
  145.7 130.6 all-reduce.5
  293.7 128.1 all-reduce.7
  486.1 130.6 all-reduce.5
  634.2 128.1 all-reduce.7
  826.7 130.6 all-reduce.5
  974.8 128.1 all-reduce.7
  1186.9 129.2 all-reduce.9
  1357.6 127.2 all-reduce.11
  1549.1 127.3 all-reduce.9
  1717.8 127.2 all-reduce.11
  1909.2 127.3 all-reduce.9
  2077.8 127.2 all-reduce.11
  2257.6 18.3 reduce-scatter.26
  2278.9 20.2 reduce-scatter.28
  2302.2 23.7 reduce-scatter.20
  2328.6 30.9 reduce-scatter.18
  2362.0 34.7 reduce-scatter.22
  2399.3 34.7 reduce-scatter.24
where the time goes:
time: 2450 us; the launch traced here: 2440 us
  waiting for transfers between devices  1730 us (71%)
  matrix products  218 us (9%)
  other arithmetic  196 us (8%)
  local copies, waits for them, and re-layouts  184 us (8%)
  blocking collectives  46.4 us (2%)
  loops' own time  41.8 us (2%)
    psum x3, waiting for transfers between devices, layer_forward(): hidden = token_rows + lax.psum(attn_term, 'tensor') + shift_rows[1]  392 us
    psum x3, waiting for transfers between devices, layer_forward(): lax.psum(mlp_term, 'tensor')  373 us
    psum x3, waiting for transfers between devices, layer_backward(): grad_normed_two = lax.psum(two_term, 'tensor')  343 us
    psum x3, waiting for transfers between devices, layer_backward(): grad_normed_one = lax.psum(one_term, 'tensor')  315 us
    ppermute x6, waiting for transfers between devices, from_behind(): lax.ppermute(value, axis, [(source, source + steps) for source in range(l...  193 us
    unnamed x15, waiting for transfers between devices  80.8 us
    dynamic_update_slice x27, other arithmetic, per_device(): lax.scan(forward_tick, jnp.zeros_like(images[0]), ticks)[1]  69.8 us
  transfers between devices with their start and end apart: 27, of which 23 were waited for; matrix products, arithmetic and copies ran while one was open for 11% of the time, Pallas kernels for 0%

commit v1 on v0

--- a/solution.py
+++ b/solution.py
@@ -7,6 +7,15 @@
 NORM_EPS = 1e-06
 GELU_ROOT = 0.7978845608028654
 GELU_CUBIC = 0.044715
+
+
+def added_up(x, mesh_axis):
+    n_dev = lax.axis_size(mesh_axis)
+    result, far = (x, 1)
+    while far < n_dev:
+        result = result + lax.ppermute(result, mesh_axis, [(i, i ^ far) for i in range(n_dev)])
+        far = 2 * far
+    return result
 
 
 def from_behind(value, axis, steps):
@@ -193,7 +202,7 @@
     )
     one_term = jnp.einsum("cte,cde->td", grad_proj, qkv_weight, preferred_element_type=jnp.float32)
     token_rows = layer_input.astype(jnp.float32).reshape(-1, model_width)
-    grad_normed_one = lax.psum(one_term, "tensor")
+    grad_normed_one = added_up(one_term, "tensor")
     centred_one, inverse_one = norm_forward(token_rows, gain_rows[0], shift_rows[0])[1:]
     from_one, gain_one_grad, shift_one_grad = norm_backward(
         grad_normed_one, centred_one, inverse_one, gain_rows[0]

time: 2450 us -> 2740 us (1.12)
  waiting for transfers between devices: 1730 us -> 2010 us
    ppermute x0 -> x6, waiting for transfers between devices: none -> 597 us  [added_up(): lax.ppermute(result, mesh_axis, [(i, i ^ far) for i in range(n_dev)])]
    psum x3 -> x0, waiting for transfers between devices: 315 us -> none  [layer_backward(): grad_normed_one = lax.psum(one_term, 'tensor')]
  transfers between devices with their start and end apart: 27 -> 30, of which waited for: 23 -> 26; matrix products, arithmetic and copies ran while one was open for 11% -> 10% of each run, Pallas kernels for 0% -> 0%
where the time goes in v1:
time: 2740 us; the launch traced here: 2730 us
  waiting for transfers between devices  2010 us (73%)
  matrix products  213 us (8%)
  other arithmetic  204 us (7%)
  local copies, waits for them, and re-layouts  184 us (7%)
  blocking collectives  46.6 us (2%)
  loops' own time  41.7 us (2%)
    ppermute x6, waiting for transfers between devices, added_up(): lax.ppermute(result, mesh_axis, [(i, i ^ far) for i in range(n_dev)])  597 us
    psum x3, waiting for transfers between devices, layer_forward(): hidden = token_rows + lax.psum(attn_term, 'tensor') + shift_rows[1]  392 us
    psum x3, waiting for transfers between devices, layer_forward(): lax.psum(mlp_term, 'tensor')  373 us
    psum x3, waiting for transfers between devices, layer_backward(): grad_normed_two = lax.psum(two_term, 'tensor')  343 us
    ppermute x6, waiting for transfers between devices, from_behind(): lax.ppermute(value, axis, [(source, source + steps) for source in range(l...  194 us
    unnamed x15, waiting for transfers between devices  80.5 us
    dynamic_update_slice x27, other arithmetic, per_device(): lax.scan(forward_tick, jnp.zeros_like(images[0]), ticks)[1]  69.7 us
  transfers between devices with their start and end apart: 30, of which 26 were waited for; matrix products, arithmetic and copies ran while one was open for 10% of the time, Pallas kernels for 0%

profile of v1, /device:TPU:0, one launch (start us, length us, event | category | flops | bytes accessed | tf_op | source)
XLA Modules:
  0.0 2734.5 jit_solution(2380726371527977574)
XLA Ops:
  112.5 1034.4 %while.66 = (s32[]{:T(128)}, bf16[1,729,1152]{2,1,0:T(8,128)(2,1)}, bf16[3,1,729,1152]{3,2,1,0:T(8,128)(2,1)}, bf16[3,1,729,1152]{3,2,1,0:T(8,128)(2,1)}, bf16[3...) while((s32[]{:T(128)}, bf16[1,729,1152]{2,1,0:T(8,128)(2,1)}, ...), condition=%wide.region_9.10_spmd, body=%wide.region_0.9_spmd.sunk | while | flops 6232035840 | bytes 263704656 | solution.py:256
  145.6 130.7 %all-reduce.5.cloned.1.call-done = f32[729,1152]{1,0:T(8,128)} async-done(((f32[729,1152]{1,0:T(8,128)}), f32[729,1152]{1,0:T(8,128)}) %all-reduce.5.cloned.1.call-update) | async-done | bytes 3359248 | tf_op jit(solution)/shard_map/while/body/eval_jaxpr/psum | solution.py:95
  297.6 124.3 %all-reduce.7.cloned.1.call-done = f32[729,1152]{1,0:T(8,128)} async-done(((f32[729,1152]{1,0:T(8,128)}), f32[729,1152]{1,0:T(8,128)}) %all-reduce.7.cloned.1.call-update) | async-done | bytes 3359248 | tf_op jit(solution)/shard_map/while/body/eval_jaxpr/psum | solution.py:102
  436.2 29.8 %collective-permute-done = bf16[1,729,1152]{2,1,0:T(8,128)(2,1)} collective-permute-done((bf16[1,729,1152]{2,1,0:T(8,128)(2,1)}, bf16[1,729,1152]{2,1,0:T(8,128)(2,1)}, u32[]{:S(2)}, u32[]{:S(2)}) %collective-permute-start) | collective-permute-done | bytes 1679648 | tf_op jit(solution)/shard_map/while/body/eval_jaxpr/ppermute | solution.py:24
  486.1 130.7 %all-reduce.5.cloned.1.call-done = f32[729,1152]{1,0:T(8,128)} async-done(((f32[729,1152]{1,0:T(8,128)}), f32[729,1152]{1,0:T(8,128)}) %all-reduce.5.cloned.1.call-update) | async-done | bytes 3359248 | tf_op jit(solution)/shard_map/while/body/eval_jaxpr/psum | solution.py:95
  638.0 124.3 %all-reduce.7.cloned.1.call-done = f32[729,1152]{1,0:T(8,128)} async-done(((f32[729,1152]{1,0:T(8,128)}), f32[729,1152]{1,0:T(8,128)}) %all-reduce.7.cloned.1.call-update) | async-done | bytes 3359248 | tf_op jit(solution)/shard_map/while/body/eval_jaxpr/psum | solution.py:102
  826.6 130.8 %all-reduce.5.cloned.1.call-done = f32[729,1152]{1,0:T(8,128)} async-done(((f32[729,1152]{1,0:T(8,128)}), f32[729,1152]{1,0:T(8,128)}) %all-reduce.5.cloned.1.call-update) | async-done | bytes 3359248 | tf_op jit(solution)/shard_map/while/body/eval_jaxpr/psum | solution.py:95
  978.6 124.3 %all-reduce.7.cloned.1.call-done = f32[729,1152]{1,0:T(8,128)} async-done(((f32[729,1152]{1,0:T(8,128)}), f32[729,1152]{1,0:T(8,128)}) %all-reduce.7.cloned.1.call-update) | async-done | bytes 3359248 | tf_op jit(solution)/shard_map/while/body/eval_jaxpr/psum | solution.py:102
  1149.8 1394.6 %while.67 = (s32[]{:T(128)}, f32[729,1152]{1,0:T(8,128)S(1)}, f32[3,1152,288]{1,2,0:T(8,128)}, f32[288,1152]{1,0:T(8,128)}, f32[1152,1076]{0,1:T(8,128)}, /*inde...) while((s32[]{:T(128)}, f32[729,1152]{1,0:T(8,128)S(1)}, ...), condition=%wide.region_30.31_spmd.clone, body=%wide.region_10.30_spmd.clone.sunk | while | flops 12739572736 | bytes 500847136 | solution.py:288
  1200.5 115.7 %all-reduce.9.cloned.1.call-done = f32[729,1152]{1,0:T(8,128)} async-done(((f32[729,1152]{1,0:T(8,128)}), f32[729,1152]{1,0:T(8,128)}) %all-reduce.9.cloned.1.call-update) | async-done | bytes 3359248 | tf_op jit(solution)/shard_map/while/body/eval_jaxpr/psum | solution.py:147
  1355.7 74.9 %collective-permute-done.1 = f32[729,1152]{1,0:T(8,128)S(1)} collective-permute-done((f32[729,1152]{1,0:T(8,128)S(1)}, f32[729,1152]{1,0:T(8,128)S(1)}, u32[]{:S(2)}, u32[]{:S(2)}) %collective-permute-start.1) | collective-permute-done | bytes 3359264 | tf_op jit(solution)/shard_map/while/body/eval_jaxpr/ppermute | solution.py:16
  1455.4 125.5 %collective-permute-done.2 = f32[729,1152]{1,0:T(8,128)} collective-permute-done((f32[729,1152]{1,0:T(8,128)}, f32[729,1152]{1,0:T(8,128)}, u32[]{:S(2)}, u32[]{:S(2)}) %collective-permute-start.2) | collective-permute-done | bytes 3359264 | tf_op jit(solution)/shard_map/while/body/eval_jaxpr/ppermute | solution.py:16
  1595.1 35.0 %collective-permute-done.3 = bf16[1,729,1152]{2,1,0:T(8,128)(2,1)S(1)} collective-permute-done((bf16[1,729,1152]{2,1,0:T(8,128)(2,1)S(1)}, bf16[1,729,1152]{2,1,0:T(8,128)(2,1)S(1)}, u32[]{:S(2)}, u32[]{:S(2)}) %collective-permute-start.3) | collective-permute-done | bytes 1679648 | tf_op jit(solution)/shard_map/while/body/eval_jaxpr/ppermute | solution.py:24
  1659.6 113.5 %all-reduce.9.cloned.1.call-done = f32[729,1152]{1,0:T(8,128)} async-done(((f32[729,1152]{1,0:T(8,128)}), f32[729,1152]{1,0:T(8,128)}) %all-reduce.9.cloned.1.call-update) | async-done | bytes 3359248 | tf_op jit(solution)/shard_map/while/body/eval_jaxpr/psum | solution.py:147
  1812.6 74.9 %collective-permute-done.1 = f32[729,1152]{1,0:T(8,128)S(1)} collective-permute-done((f32[729,1152]{1,0:T(8,128)S(1)}, f32[729,1152]{1,0:T(8,128)S(1)}, u32[]{:S(2)}, u32[]{:S(2)}) %collective-permute-start.1) | collective-permute-done | bytes 3359264 | tf_op jit(solution)/shard_map/while/body/eval_jaxpr/ppermute | solution.py:16
  1914.3 123.5 %collective-permute-done.2 = f32[729,1152]{1,0:T(8,128)} collective-permute-done((f32[729,1152]{1,0:T(8,128)}, f32[729,1152]{1,0:T(8,128)}, u32[]{:S(2)}, u32[]{:S(2)}) %collective-permute-start.2) | collective-permute-done | bytes 3359264 | tf_op jit(solution)/shard_map/while/body/eval_jaxpr/ppermute | solution.py:16
  2051.9 35.0 %collective-permute-done.3 = bf16[1,729,1152]{2,1,0:T(8,128)(2,1)S(1)} collective-permute-done((bf16[1,729,1152]{2,1,0:T(8,128)(2,1)S(1)}, bf16[1,729,1152]{2,1,0:T(8,128)(2,1)S(1)}, u32[]{:S(2)}, u32[]{:S(2)}) %collective-permute-start.3) | collective-permute-done | bytes 1679648 | tf_op jit(solution)/shard_map/while/body/eval_jaxpr/ppermute | solution.py:24
  2116.4 113.5 %all-reduce.9.cloned.1.call-done = f32[729,1152]{1,0:T(8,128)} async-done(((f32[729,1152]{1,0:T(8,128)}), f32[729,1152]{1,0:T(8,128)}) %all-reduce.9.cloned.1.call-update) | async-done | bytes 3359248 | tf_op jit(solution)/shard_map/while/body/eval_jaxpr/psum | solution.py:147
  2269.3 74.9 %collective-permute-done.1 = f32[729,1152]{1,0:T(8,128)S(1)} collective-permute-done((f32[729,1152]{1,0:T(8,128)S(1)}, f32[729,1152]{1,0:T(8,128)S(1)}, u32[]{:S(2)}, u32[]{:S(2)}) %collective-permute-start.1) | collective-permute-done | bytes 3359264 | tf_op jit(solution)/shard_map/while/body/eval_jaxpr/ppermute | solution.py:16
  2370.9 123.5 %collective-permute-done.2 = f32[729,1152]{1,0:T(8,128)} collective-permute-done((f32[729,1152]{1,0:T(8,128)}, f32[729,1152]{1,0:T(8,128)}, u32[]{:S(2)}, u32[]{:S(2)}) %collective-permute-start.2) | collective-permute-done | bytes 3359264 | tf_op jit(solution)/shard_map/while/body/eval_jaxpr/ppermute | solution.py:16
  2508.7 35.0 %collective-permute-done.3 = bf16[1,729,1152]{2,1,0:T(8,128)(2,1)S(1)} collective-permute-done((bf16[1,729,1152]{2,1,0:T(8,128)(2,1)S(1)}, bf16[1,729,1152]{2,1,0:T(8,128)(2,1)S(1)}, u32[]{:S(2)}, u32[]{:S(2)}) %collective-permute-start.3) | collective-permute-done | bytes 1679648 | tf_op jit(solution)/shard_map/while/body/eval_jaxpr/ppermute | solution.py:24
  2587.0 31.6 %rev.4 = bf16[2,1,729,1152]{3,0,2,1:T(2,128)(2,1)} reverse(bf16[2,1,729,1152]{3,0,2,1:T(2,128)(2,1)} %constant_dynamic-slice_fusion.3), dimensions={0} | reverse | bytes 6718464 | tf_op jit(solution)/shard_map/jit(_flip)/rev | solution.py:312
  2655.1 32.0 %reduce-scatter.23.cloned.1.call-done = bf16[288,1076]{1,0:T(8,128)(2,1)} async-done(((bf16[1152,1076]{1,0:T(8,128)(2,1)}), bf16[288,1076]{1,0:T(8,128)(2,1)}) %reduce-scatter.23.cloned.1.call-update) | async-done | bytes 619792
  2690.3 34.0 %reduce-scatter.25.cloned.1.call-done = bf16[288,1076]{1,0:T(8,128)(2,1)} async-done(((bf16[1152,1076]{1,0:T(8,128)(2,1)}), bf16[288,1076]{1,0:T(8,128)(2,1)}) %reduce-scatter.25.cloned.1.call-update) | async-done | bytes 619792
  (798 shorter events, 740.3 us)
Async XLA Ops:
  7.2 58.4 %all-gather.10.cloned.1.call-start = ((), (), s32[]{:S(2)}) async-start(), calls=%async_computation.6 | async-start | bytes 4423680 | tf_op jit(solution)/shard_map/all_gather | solution.py:237
  9.8 68.9 %all-gather.14.cloned.1.call-start = ((), (), s32[]{:S(2)}) async-start(), calls=%async_computation.8 | async-start | bytes 3317760 | tf_op jit(solution)/shard_map/all_gather | solution.py:240
  10.5 95.4 %all-gather.12.cloned.1.call-start = ((), (), s32[]{:S(2)}) async-start(), calls=%async_computation.7 | async-start | bytes 3317760 | tf_op jit(solution)/shard_map/all_gather | solution.py:239
  125.5 150.8 %all-reduce.5.cloned.1.call-start = ((), (), s32[]{:S(2)}) async-start(), calls=%async_computation.15 | async-start | bytes 6782976 | tf_op jit(solution)/shard_map/while/body/eval_jaxpr/psum | solution.py:95
  145.6 276.4 %all-reduce.7.cloned.1.call-start = ((), (), s32[]{:S(2)}) async-start(), calls=%async_computation.16 | async-start | bytes 6782976 | tf_op jit(solution)/shard_map/while/body/eval_jaxpr/psum | solution.py:102
  466.0 150.8 %all-reduce.5.cloned.1.call-start = ((), (), s32[]{:S(2)}) async-start(), calls=%async_computation.15 | async-start | bytes 6782976 | tf_op jit(solution)/shard_map/while/body/eval_jaxpr/psum | solution.py:95
  486.0 276.4 %all-reduce.7.cloned.1.call-start = ((), (), s32[]{:S(2)}) async-start(), calls=%async_computation.16 | async-start | bytes 6782976 | tf_op jit(solution)/shard_map/while/body/eval_jaxpr/psum | solution.py:102
  806.5 150.8 %all-reduce.5.cloned.1.call-start = ((), (), s32[]{:S(2)}) async-start(), calls=%async_computation.15 | async-start | bytes 6782976 | tf_op jit(solution)/shard_map/while/body/eval_jaxpr/psum | solution.py:95
  826.5 276.4 %all-reduce.7.cloned.1.call-start = ((), (), s32[]{:S(2)}) async-start(), calls=%async_computation.16 | async-start | bytes 6782976 | tf_op jit(solution)/shard_map/while/body/eval_jaxpr/psum | solution.py:102
  1171.3 144.9 %all-reduce.9.cloned.1.call-start = ((), (), s32[]{:S(2)}) async-start(), calls=%async_computation.17 | async-start | bytes 6782976 | tf_op jit(solution)/shard_map/while/body/eval_jaxpr/psum | solution.py:147
  1355.7 75.0 %collective-permute-start.1 = (f32[729,1152]{1,0:T(8,128)S(1)}, f32[729,1152]{1,0:T(8,128)S(1)}, u32[]{:S(2)}, u32[]{:S(2)}) collective-permute-start(f32[729,1152]{1,0:T(8,128)S(1)} %convolution_bitcast_fusion.5), channel_id=1, source_target_pairs={{0,4},{4,0},{8,12},{12,8},{1,5},{5,1},{9,13},{13,9},{2,6},{6,2},{1... | collective-permute-start | bytes 10077704 | tf_op jit(solution)/shard_map/while/body/eval_jaxpr/ppermute | solution.py:16
  1432.9 148.0 %collective-permute-start.2 = (f32[729,1152]{1,0:T(8,128)}, f32[729,1152]{1,0:T(8,128)}, u32[]{:S(2)}, u32[]{:S(2)}) collective-permute-start(f32[729,1152]{1,0:T(8,128)} %add.588), channel_id=1, source_target_pairs={{0,8},{4,12},{8,0},{12,4},{1,9},{5,13},{9,1},{13,5},{2,10},{6,14},... | collective-permute-start | bytes 10077704 | tf_op jit(solution)/shard_map/while/body/eval_jaxpr/ppermute | solution.py:16
  1630.3 142.8 %all-reduce.9.cloned.1.call-start = ((), (), s32[]{:S(2)}) async-start(), calls=%async_computation.17 | async-start | bytes 6782976 | tf_op jit(solution)/shard_map/while/body/eval_jaxpr/psum | solution.py:147
  1812.6 75.0 %collective-permute-start.1 = (f32[729,1152]{1,0:T(8,128)S(1)}, f32[729,1152]{1,0:T(8,128)S(1)}, u32[]{:S(2)}, u32[]{:S(2)}) collective-permute-start(f32[729,1152]{1,0:T(8,128)S(1)} %convolution_bitcast_fusion.5), channel_id=1, source_target_pairs={{0,4},{4,0},{8,12},{12,8},{1,5},{5,1},{9,13},{13,9},{2,6},{6,2},{1... | collective-permute-start | bytes 10077704 | tf_op jit(solution)/shard_map/while/body/eval_jaxpr/ppermute | solution.py:16
  1889.8 148.0 %collective-permute-start.2 = (f32[729,1152]{1,0:T(8,128)}, f32[729,1152]{1,0:T(8,128)}, u32[]{:S(2)}, u32[]{:S(2)}) collective-permute-start(f32[729,1152]{1,0:T(8,128)} %add.588), channel_id=1, source_target_pairs={{0,8},{4,12},{8,0},{12,4},{1,9},{5,13},{9,1},{13,5},{2,10},{6,14},... | collective-permute-start | bytes 10077704 | tf_op jit(solution)/shard_map/while/body/eval_jaxpr/ppermute | solution.py:16
  2087.2 142.8 %all-reduce.9.cloned.1.call-start = ((), (), s32[]{:S(2)}) async-start(), calls=%async_computation.17 | async-start | bytes 6782976 | tf_op jit(solution)/shard_map/while/body/eval_jaxpr/psum | solution.py:147
  2269.2 75.0 %collective-permute-start.1 = (f32[729,1152]{1,0:T(8,128)S(1)}, f32[729,1152]{1,0:T(8,128)S(1)}, u32[]{:S(2)}, u32[]{:S(2)}) collective-permute-start(f32[729,1152]{1,0:T(8,128)S(1)} %convolution_bitcast_fusion.5), channel_id=1, source_target_pairs={{0,4},{4,0},{8,12},{12,8},{1,5},{5,1},{9,13},{13,9},{2,6},{6,2},{1... | collective-permute-start | bytes 10077704 | tf_op jit(solution)/shard_map/while/body/eval_jaxpr/ppermute | solution.py:16
  2346.5 148.0 %collective-permute-start.2 = (f32[729,1152]{1,0:T(8,128)}, f32[729,1152]{1,0:T(8,128)}, u32[]{:S(2)}, u32[]{:S(2)}) collective-permute-start(f32[729,1152]{1,0:T(8,128)} %add.588), channel_id=1, source_target_pairs={{0,8},{4,12},{8,0},{12,4},{1,9},{5,13},{9,1},{13,5},{2,10},{6,14},... | collective-permute-start | bytes 10077704 | tf_op jit(solution)/shard_map/while/body/eval_jaxpr/ppermute | solution.py:16
  2544.4 87.5 %reduce-scatter.27.cloned.1.call-start = ((), (), s32[]{:S(2)}) async-start(), calls=%async_computation.13 | async-start | bytes 368640
  2545.4 88.1 %reduce-scatter.29.cloned.1.call-start = ((), (), s32[]{:S(2)}) async-start(), calls=%async_computation.14 | async-start | bytes 368640
  2546.4 88.6 %reduce-scatter.21.cloned.1.call-start = ((), (), s32[]{:S(2)}) async-start(), calls=%async_computation.10 | async-start | bytes 1105920
  2549.1 100.9 %reduce-scatter.19.cloned.1.call-start = ((), (), s32[]{:S(2)}) async-start(), calls=%async_computation.9 | async-start | bytes 2580480
  2563.0 124.2 %reduce-scatter.23.cloned.1.call-start = ((), (), s32[]{:S(2)}) async-start(), calls=%async_computation.11 | async-start | bytes 3317760
  2569.0 155.3 %reduce-scatter.25.cloned.1.call-start = ((), (), s32[]{:S(2)}) async-start(), calls=%async_computation.12 | async-start | bytes 3317760
  (210 other events, 2301.0 us)
Sparse Core Ops, SparseCore 0:
  10.1 40.3 all-gather.9
  52.1 26.5 all-gather.13
  80.2 25.7 all-gather.11
  145.7 130.6 all-reduce.4
  293.7 128.1 all-reduce.6
  486.1 130.6 all-reduce.4
  634.2 128.1 all-reduce.6
  826.6 130.6 all-reduce.4
  974.7 128.1 all-reduce.6
  1186.9 129.2 all-reduce.8
  1645.9 127.1 all-reduce.8
  2102.8 127.1 all-reduce.8
  2548.3 18.1 reduce-scatter.26
  2569.4 20.2 reduce-scatter.28
  2592.7 23.8 reduce-scatter.20
  2619.0 30.9 reduce-scatter.18
  2652.4 34.6 reduce-scatter.22
  2689.5 34.7 reduce-scatter.24
